TPU v7x, 512 devices: a whole 4x8x8 slice. The times are simulated.
512 devices in a mesh: lon: 32 (over z, x), lat: 16 (over y, core).
Axes of the slice: x: 4, y: 8, z: 8, core: 2. Of those that a mesh axis runs over, the one named last changes fastest.
Arguments:
- right_side: float32 [2, 32, 256, 4096], P(None, None, 'lat', 'lon'), may hold values from -36 to 36
- sea_mask: int32 [32, 256, 4096], P(None, 'lat', 'lon'), may hold values 0 or 1
- levels: int32 [256, 4096], P('lat', 'lon'), may hold values from 0 to 32
- east_diffusivity: bfloat16 [32, 256, 4096], P(None, 'lat', 'lon'), may hold values from 1 to 8
- north_diffusivity: bfloat16 [32, 256, 4096], P(None, 'lat', 'lon'), may hold values from 1 to 8
- vertical_diffusivity: bfloat16 [32, 256, 4096], P(None, 'lat', 'lon'), may hold values from 0.5 to 8
Outputs:
- solution_field: float32 [2, 32, 256, 4096], P(None, None, 'lat', 'lon')
- residual: float32 [2, 32, 256, 4096], P(None, None, 'lat', 'lon')
All inputs are finite; a program needn't handle non-finite values. No bound on the sum of `sea_mask` on one device may be relied on, other than what follows from the above.
Results may differ from a plain program's by a relative error of at most 0.004.
Values sent between devices are 32-bit elements; how exact they have to be, the bound alone decides.
A program may use at most 64 MiB of HBM per device.

v0:
```python
import jax
import jax.numpy as jnp
from jax import lax
from jax.sharding import PartitionSpec as P

ITERS = 2


def from_behind(x, axis, by):
    devices = lax.axis_size(axis)
    return lax.ppermute(x, axis, [(i, (i + by) % devices) for i in range(devices)])


def shifted(x, axis, by):
    devices = lax.axis_size(axis)
    pairs = [(i, i + by) for i in range(devices) if 0 <= i + by < devices]
    return lax.ppermute(x, axis, pairs)


def local_sum(first, second):
    return jnp.sum(first * second, axis=(1, 2, 3))


def expand(scalars):
    return scalars[:, None, None, None]


def vertical_change(field, coef_down):
    value_below = jnp.concatenate([field[:, 1:], jnp.zeros_like(field[:, :1])], axis=1)
    flux_down = coef_down * (value_below - field)
    flux_above = jnp.concatenate([jnp.zeros_like(flux_down[:, :1]), flux_down[:, :-1]], axis=1)
    return flux_above - flux_down


def body(right_side, sea_mask, levels, east_diffusivity, north_diffusivity, vertical_diffusivity):
    depth_index = lax.broadcasted_iota(jnp.int32, sea_mask.shape, 0)
    ocean_flag = ((sea_mask == 1) & (depth_index < levels[None])).astype(jnp.int32)
    east_column = from_behind(ocean_flag[:, :, :1], "lon", -1)
    north_row = shifted(ocean_flag[:, :1, :], "lat", -1)
    ocean = ocean_flag.astype(jnp.float32)
    ocean_east = jnp.concatenate([ocean[:, :, 1:], east_column.astype(jnp.float32)], axis=2)
    ocean_north = jnp.concatenate([ocean[:, 1:, :], north_row.astype(jnp.float32)], axis=1)
    ocean_below = jnp.concatenate([ocean[1:], jnp.zeros_like(ocean[:1])], axis=0)
    coef_east = east_diffusivity.astype(jnp.float32) * ocean * ocean_east
    coef_north = north_diffusivity.astype(jnp.float32) * ocean * ocean_north
    coef_down = vertical_diffusivity.astype(jnp.float32) * ocean * ocean_below
    solution = jnp.zeros_like(right_side)
    residual = right_side

    def sum_squares(field):
        return lax.psum(local_sum(field, field), ("lon", "lat"))

    direction = right_side
    norm_now = sum_squares(residual)
    for iteration in range(ITERS):
        first_column = from_behind(direction[:, :, :, :1], "lon", -1)
        first_row = shifted(direction[:, :, :1, :], "lat", -1)
        value_east = jnp.concatenate([direction[:, :, :, 1:], first_column], axis=3)
        value_north = jnp.concatenate([direction[:, :, 1:, :], first_row], axis=2)
        flux_east = coef_east * (value_east - direction)
        flux_north = coef_north * (value_north - direction)
        last_column = from_behind(flux_east[:, :, :, -1:], "lon", 1)
        last_row = shifted(flux_north[:, :, -1:, :], "lat", 1)
        flux_west = jnp.concatenate([last_column, flux_east[:, :, :, :-1]], axis=3)
        flux_south = jnp.concatenate([last_row, flux_north[:, :, :-1, :]], axis=2)
        image = (
            direction
            + (flux_west - flux_east)
            + (flux_south - flux_north)
            + vertical_change(direction, coef_down)
        )
        step_size = norm_now / lax.psum(local_sum(direction, image), ("lon", "lat"))
        solution = solution + expand(step_size) * direction
        residual = residual - expand(step_size) * image
        norm_next = sum_squares(residual)
        direction = residual + expand(norm_next / norm_now) * direction
        norm_now = norm_next
    return (solution, residual)


def solution(mesh):
    return jax.shard_map(
        body,
        mesh=mesh,
        in_specs=(
            P(None, None, "lat", "lon"),
            P(None, "lat", "lon"),
            P("lat", "lon"),
            P(None, "lat", "lon"),
            P(None, "lat", "lon"),
            P(None, "lat", "lon"),
        ),
        out_specs=(P(None, None, "lat", "lon"), P(None, None, "lat", "lon")),
        check_vma=False,
    )
```

profile of v0, /device:TPU:1, one launch (start us, length us, event | category | flops | bytes accessed | tf_op | source)
XLA Modules:
  0.0 386.5 jit_solution(15036093700359671659)
XLA Ops:
  0.6 1.1 fusion.14
  1.7 8.8 %collective-permute-start.3 = (s32[32,1,128]{2,1,0:T(1,128)S(1)}, s32[32,1,128]{2,1,0:T(1,128)S(1)}, u32[]{:S(2)}, u32[]{:S(2)}) collective-permute-start(s32[32,1,128]{2,1,0:T(1,128)S(1)} %slice.105), channel_id=1, source_target_pairs={{1,0},{2,1},{3,2},{4,3},{5,4},{6,5},{7,6},{8,7},{9,8},{10,9},{11,1... | collective-permute-start | bytes 49160 | tf_op jit(solution)/shard_map/ppermute | solution.py:17
  10.5 7.5 %collective-permute-start = (s32[32,16,1]{2,1,0:T(8,128)S(1)}, s32[32,16,1]{2,1,0:T(8,128)S(1)}, u32[]{:S(2)}, u32[]{:S(2)}) collective-permute-start(s32[32,16,1]{2,1,0:T(8,128)S(1)} %bitcast.13), channel_id=1, source_target_pairs={{0,496},{16,0},{32,16},{48,32},{64,48},{80,64},{96,80},{112,96},{1... | collective-permute-start | bytes 6152 | tf_op jit(solution)/shard_map/ppermute | solution.py:11
  18.1 1.9 collective-permute-start.4
  20.0 2.5 collective-permute-start.1
  22.6 0.2 slice.77
  22.8 0.1 slice.100
  23.0 1.2 collective-permute-done
  24.2 0.2 maximum_multiply_fusion
  24.4 10.9 %collective-permute-done.1 = f32[2,32,16,1]{3,2,1,0:T(8,128)S(1)} collective-permute-done((f32[2,32,16,1]{3,2,1,0:T(8,128)S(1)}, f32[2,32,16,1]{3,2,1,0:T(8,128)S(1)}, u32[]{:S(2)}, u32[]{:S(2)}) %collective-permute-start.1) | collective-permute-done | bytes 4128 | tf_op jit(solution)/shard_map/ppermute | solution.py:11
  35.3 0.4 fusion
  35.7 4.3 %collective-permute-start.5 = (f32[2,32,1,128]{3,2,1,0:T(1,128)S(1)}, f32[2,32,1,128]{3,2,1,0:T(1,128)S(1)}, u32[]{:S(2)}, u32[]{:S(2)}) collective-permute-start(f32[2,32,1,128]{3,2,1,0:T(1,128)S(1)} %slice.106), channel_id=1, source_target_pairs={{0,1},{1,2},{2,3},{3,4},{4,5},{5,6},{6,7},{7,8},{8,9},{9,10},{10,1... | collective-permute-start | bytes 98312 | tf_op jit(solution)/shard_map/ppermute | solution.py:17
  40.0 0.2 slice.102
  40.2 1.9 collective-permute-start.2
  42.2 15.7 %collective-permute-done.2 = f32[2,32,16,1]{3,2,1,0:T(8,128)S(1)} collective-permute-done((f32[2,32,16,1]{3,2,1,0:T(8,128)S(1)}, f32[2,32,16,1]{3,2,1,0:T(8,128)S(1)}, u32[]{:S(2)}, u32[]{:S(2)}) %collective-permute-start.2) | collective-permute-done | bytes 4128 | tf_op jit(solution)/shard_map/ppermute | solution.py:11
  57.9 0.5 multiply_reduce_fusion.2
  58.4 97.2 %all-reduce.5 = (f32[2]{0:T(128)S(1)}, f32[2]{0:T(128)S(1)}) all-reduce(f32[2]{0:T(128)S(1)} %get-tuple-element.3, f32[2]{0:T(128)S(1)} %get-tuple-element.2), channel_id=1, replica_groups=mesh['lon'=32,'lat'=16] {'lon','lat'}, use_global_device_ids=true, to_apply=%region_1.0 | all-reduce | flops 4 | bytes 32 | tf_op jit(solution)/shard_map/psum | solution.py:51
  155.6 0.3 multiply_reduce_fusion.1
  155.9 94.4 %psum.30 = f32[2]{0:T(128)S(1)} all-reduce(f32[2]{0:T(128)S(1)} %multiply_reduce_fusion.1), channel_id=1, replica_groups=mesh['lon'=32,'lat'=16] {'lon','lat'}, use_global_device_ids=true, to_apply=%region_5.0 | all-reduce | flops 2 | bytes 16 | tf_op jit(solution)/shard_map/psum | solution.py:51
  250.3 0.1 multiply_add_fusion.1
  250.5 2.6 collective-permute-start.8
  253.1 4.5 %collective-permute-start.6 = (f32[2,32,16,1]{3,2,1,0:T(8,128)S(1)}, f32[2,32,16,1]{3,2,1,0:T(8,128)S(1)}, u32[]{:S(2)}, u32[]{:S(2)}) collective-permute-start(f32[2,32,16,1]{3,2,1,0:T(8,128)S(1)} %bitcast.8), channel_id=1, source_target_pairs={{0,496},{16,0},{32,16},{48,32},{64,48},{80,64},{96,80},{112,96},{1... | collective-permute-start | bytes 12296 | tf_op jit(solution)/shard_map/ppermute | solution.py:11
  257.7 0.2 slice.110
  257.9 11.3 %collective-permute-done.6 = f32[2,32,16,1]{3,2,1,0:T(8,128)S(1)} collective-permute-done((f32[2,32,16,1]{3,2,1,0:T(8,128)S(1)}, f32[2,32,16,1]{3,2,1,0:T(8,128)S(1)}, u32[]{:S(2)}, u32[]{:S(2)}) %collective-permute-start.6) | collective-permute-done | bytes 4128 | tf_op jit(solution)/shard_map/ppermute | solution.py:11
  269.2 0.4 fusion.5
  269.6 2.6 collective-permute-start.9
  272.2 0.2 slice.112
  272.4 2.8 collective-permute-start.7
  275.3 15.8 %collective-permute-done.7 = f32[2,32,16,1]{3,2,1,0:T(8,128)S(1)} collective-permute-done((f32[2,32,16,1]{3,2,1,0:T(8,128)S(1)}, f32[2,32,16,1]{3,2,1,0:T(8,128)S(1)}, u32[]{:S(2)}, u32[]{:S(2)}) %collective-permute-start.7) | collective-permute-done | bytes 4128 | tf_op jit(solution)/shard_map/ppermute | solution.py:11
  291.1 0.5 multiply_reduce_fusion
  291.6 93.8 %psum.31 = f32[2]{0:T(128)S(1)} all-reduce(f32[2]{0:T(128)S(1)} %get-tuple-element.6), channel_id=1, replica_groups=mesh['lon'=32,'lat'=16] {'lon','lat'}, use_global_device_ids=true, to_apply=%region_7.0 | all-reduce | flops 2 | bytes 16 | tf_op jit(solution)/shard_map/psum | solution.py:72
  385.3 1.2 multiply_subtract_fusion
  (31 shorter events, 0.5 us)
Async XLA Ops:
  0.6 17.4 %copy-start = (f32[2,32,16,128]{3,2,1,0:T(8,128)S(1)}, f32[2,32,16,128]{3,2,1,0:T(8,128)}, u32[]{:S(2)}) copy-start(f32[2,32,16,128]{3,2,1,0:T(8,128)} %param.6) | copy-start | bytes 1572868
  1.7 22.4 %collective-permute-start.3 = (s32[32,1,128]{2,1,0:T(1,128)S(1)}, s32[32,1,128]{2,1,0:T(1,128)S(1)}, u32[]{:S(2)}, u32[]{:S(2)}) collective-permute-start(s32[32,1,128]{2,1,0:T(1,128)S(1)} %slice.105), channel_id=1, source_target_pairs={{1,0},{2,1},{3,2},{4,3},{5,4},{6,5},{7,6},{8,7},{9,8},{10,9},{11,1... | collective-permute-start | bytes 49160 | tf_op jit(solution)/shard_map/ppermute | solution.py:17
  10.5 13.6 %collective-permute-start = (s32[32,16,1]{2,1,0:T(8,128)S(1)}, s32[32,16,1]{2,1,0:T(8,128)S(1)}, u32[]{:S(2)}, u32[]{:S(2)}) collective-permute-start(s32[32,16,1]{2,1,0:T(8,128)S(1)} %bitcast.13), channel_id=1, source_target_pairs={{0,496},{16,0},{32,16},{48,32},{64,48},{80,64},{96,80},{112,96},{1... | collective-permute-start | bytes 6152 | tf_op jit(solution)/shard_map/ppermute | solution.py:11
  18.1 17.2 %collective-permute-start.4 = (f32[2,32,1,128]{3,2,1,0:T(1,128)S(1)}, f32[2,32,1,128]{3,2,1,0:T(1,128)S(1)}, u32[]{:S(2)}, u32[]{:S(2)}) collective-permute-start(f32[2,32,1,128]{3,2,1,0:T(1,128)S(1)} %slice.84), channel_id=1, source_target_pairs={{1,0},{2,1},{3,2},{4,3},{5,4},{6,5},{7,6},{8,7},{9,8},{10,9},{11,1... | collective-permute-start | bytes 98312 | tf_op jit(solution)/shard_map/ppermute | solution.py:17
  20.0 15.3 %collective-permute-start.1 = (f32[2,32,16,1]{3,2,1,0:T(8,128)S(1)}, f32[2,32,16,1]{3,2,1,0:T(8,128)S(1)}, u32[]{:S(2)}, u32[]{:S(2)}) collective-permute-start(f32[2,32,16,1]{3,2,1,0:T(8,128)S(1)} %bitcast.7), channel_id=1, source_target_pairs={{0,496},{16,0},{32,16},{48,32},{64,48},{80,64},{96,80},{112,96},{1... | collective-permute-start | bytes 12296 | tf_op jit(solution)/shard_map/ppermute | solution.py:11
  22.9 1.2 copy-start.1
  23.0 1.2 copy-start.2
  23.0 1.2 copy-start.3
  35.7 22.2 %collective-permute-start.5 = (f32[2,32,1,128]{3,2,1,0:T(1,128)S(1)}, f32[2,32,1,128]{3,2,1,0:T(1,128)S(1)}, u32[]{:S(2)}, u32[]{:S(2)}) collective-permute-start(f32[2,32,1,128]{3,2,1,0:T(1,128)S(1)} %slice.106), channel_id=1, source_target_pairs={{0,1},{1,2},{2,3},{3,4},{4,5},{5,6},{6,7},{7,8},{8,9},{9,10},{10,1... | collective-permute-start | bytes 98312 | tf_op jit(solution)/shard_map/ppermute | solution.py:17
  40.2 17.7 %collective-permute-start.2 = (f32[2,32,16,1]{3,2,1,0:T(8,128)S(1)}, f32[2,32,16,1]{3,2,1,0:T(8,128)S(1)}, u32[]{:S(2)}, u32[]{:S(2)}) collective-permute-start(f32[2,32,16,1]{3,2,1,0:T(8,128)S(1)} %slice.102), channel_id=1, source_target_pairs={{0,16},{16,32},{32,48},{48,64},{64,80},{80,96},{96,112},{112,128},... | collective-permute-start | bytes 12296 | tf_op jit(solution)/shard_map/ppermute | solution.py:11
  250.5 18.8 %collective-permute-start.8 = (f32[2,32,1,128]{3,2,1,0:T(1,128)S(1)}, f32[2,32,1,128]{3,2,1,0:T(1,128)S(1)}, u32[]{:S(2)}, u32[]{:S(2)}) collective-permute-start(f32[2,32,1,128]{3,2,1,0:T(1,128)S(1)} %slice.115), channel_id=1, source_target_pairs={{1,0},{2,1},{3,2},{4,3},{5,4},{6,5},{7,6},{8,7},{9,8},{10,9},{11,1... | collective-permute-start | bytes 98312 | tf_op jit(solution)/shard_map/ppermute | solution.py:17
  253.1 16.2 %collective-permute-start.6 = (f32[2,32,16,1]{3,2,1,0:T(8,128)S(1)}, f32[2,32,16,1]{3,2,1,0:T(8,128)S(1)}, u32[]{:S(2)}, u32[]{:S(2)}) collective-permute-start(f32[2,32,16,1]{3,2,1,0:T(8,128)S(1)} %bitcast.8), channel_id=1, source_target_pairs={{0,496},{16,0},{32,16},{48,32},{64,48},{80,64},{96,80},{112,96},{1... | collective-permute-start | bytes 12296 | tf_op jit(solution)/shard_map/ppermute | solution.py:11
  269.6 21.5 %collective-permute-start.9 = (f32[2,32,1,128]{3,2,1,0:T(1,128)S(1)}, f32[2,32,1,128]{3,2,1,0:T(1,128)S(1)}, u32[]{:S(2)}, u32[]{:S(2)}) collective-permute-start(f32[2,32,1,128]{3,2,1,0:T(1,128)S(1)} %slice.116), channel_id=1, source_target_pairs={{0,1},{1,2},{2,3},{3,4},{4,5},{5,6},{6,7},{7,8},{8,9},{9,10},{10,1... | collective-permute-start | bytes 98312 | tf_op jit(solution)/shard_map/ppermute | solution.py:17
  272.4 18.7 %collective-permute-start.7 = (f32[2,32,16,1]{3,2,1,0:T(8,128)S(1)}, f32[2,32,16,1]{3,2,1,0:T(8,128)S(1)}, u32[]{:S(2)}, u32[]{:S(2)}) collective-permute-start(f32[2,32,16,1]{3,2,1,0:T(8,128)S(1)} %slice.112), channel_id=1, source_target_pairs={{0,16},{16,32},{32,48},{48,64},{64,80},{80,96},{96,112},{112,128},... | collective-permute-start | bytes 12296 | tf_op jit(solution)/shard_map/ppermute | solution.py:11
where the time goes:
time: 387 us
  blocking collectives  285 us (74%)
  waiting for transfers between devices  54.9 us (14%)
  starting transfers between devices  39.4 us (10%)
  other arithmetic  4.62 us (1%)
    psum x2, blocking collectives, sum_squares(): return lax.psum(local_sum(field, field), ('lon', 'lat'))  192 us
    psum x1, blocking collectives, body(): step_size = norm_now / lax.psum(local_sum(direction, image), ('lon', 'lat'))  93.8 us
    ppermute x5, waiting for transfers between devices, from_behind(): lax.ppermute(x, axis, [(i, (i + by) % devices) for i in range(devices)])  54.9 us
    ppermute x5, starting transfers between devices, shifted(): return lax.ppermute(x, axis, pairs)  20.2 us
    ppermute x5, starting transfers between devices, from_behind(): lax.ppermute(x, axis, [(i, (i + by) % devices) for i in range(devices)])  19.2 us
  transfers between devices with their start and end apart: 10, of which 5 were waited for; matrix products, arithmetic and copies ran while one was open for 0% of the time, Pallas kernels for 0%

commit v1 on v0

--- a/solution.py
+++ b/solution.py
@@ -48,7 +48,10 @@
     residual = right_side
 
     def sum_squares(field):
-        return lax.psum(local_sum(field, field), ("lon", "lat"))
+        solve_forms = lambda incoming_x, comm_axis: jnp.sum(
+            jax.lax.all_gather(incoming_x, axis_name=comm_axis), axis=0
+        )
+        return solve_forms(local_sum(field, field), ("lon", "lat"))
 
     direction = right_side
     norm_now = sum_squares(residual)

time: 387 us -> 389 us (level)
    unnamed x0 -> x2, blocking collectives: none -> 192 us
    psum x2 -> x0, blocking collectives: 192 us -> none  [sum_squares(): return lax.psum(local_sum(field, field), ('lon', 'lat'))]
where the time goes in v1:
time: 389 us
  blocking collectives  285 us (73%)
  waiting for transfers between devices  55 us (14%)
  starting transfers between devices  39.4 us (10%)
  other arithmetic  5.76 us (1%)
    unnamed x2, blocking collectives  192 us
    psum x1, blocking collectives, body(): step_size = norm_now / lax.psum(local_sum(direction, image), ('lon', 'lat'))  93.8 us
    ppermute x5, waiting for transfers between devices, from_behind(): lax.ppermute(x, axis, [(i, (i + by) % devices) for i in range(devices)])  55 us
    ppermute x5, starting transfers between devices, shifted(): return lax.ppermute(x, axis, pairs)  20.2 us
    ppermute x5, starting transfers between devices, from_behind(): lax.ppermute(x, axis, [(i, (i + by) % devices) for i in range(devices)])  19.2 us
  transfers between devices with their start and end apart: 10, of which 5 were waited for; matrix products, arithmetic and copies ran while one was open for 0% of the time, Pallas kernels for 0%

profile of v1, /device:TPU:1, one launch (start us, length us, event | category | flops | bytes accessed | tf_op | source)
XLA Modules:
  0.0 388.7 jit_solution(4771734816059415103)
XLA Ops:
  0.6 1.1 fusion.14
  1.7 8.8 %collective-permute-start.3 = (s32[32,1,128]{2,1,0:T(1,128)S(1)}, s32[32,1,128]{2,1,0:T(1,128)S(1)}, u32[]{:S(2)}, u32[]{:S(2)}) collective-permute-start(s32[32,1,128]{2,1,0:T(1,128)S(1)} %slice.105), channel_id=1, source_target_pairs={{1,0},{2,1},{3,2},{4,3},{5,4},{6,5},{7,6},{8,7},{9,8},{10,9},{11,1... | collective-permute-start | bytes 49160 | tf_op jit(solution)/shard_map/ppermute | solution.py:17
  10.5 7.5 %collective-permute-start = (s32[32,16,1]{2,1,0:T(8,128)S(1)}, s32[32,16,1]{2,1,0:T(8,128)S(1)}, u32[]{:S(2)}, u32[]{:S(2)}) collective-permute-start(s32[32,16,1]{2,1,0:T(8,128)S(1)} %bitcast.13), channel_id=1, source_target_pairs={{0,496},{16,0},{32,16},{48,32},{64,48},{80,64},{96,80},{112,96},{1... | collective-permute-start | bytes 6152 | tf_op jit(solution)/shard_map/ppermute | solution.py:11
  18.1 1.9 collective-permute-start.4
  20.0 2.5 collective-permute-start.1
  22.6 0.2 slice.77
  23.0 1.2 collective-permute-done
  24.4 10.9 %collective-permute-done.1 = f32[2,32,16,1]{3,2,1,0:T(8,128)S(1)} collective-permute-done((f32[2,32,16,1]{3,2,1,0:T(8,128)S(1)}, f32[2,32,16,1]{3,2,1,0:T(8,128)S(1)}, u32[]{:S(2)}, u32[]{:S(2)}) %collective-permute-start.1) | collective-permute-done | bytes 4128 | tf_op jit(solution)/shard_map/ppermute | solution.py:11
  35.3 0.4 fusion
  35.7 4.3 %collective-permute-start.5 = (f32[2,32,1,128]{3,2,1,0:T(1,128)S(1)}, f32[2,32,1,128]{3,2,1,0:T(1,128)S(1)}, u32[]{:S(2)}, u32[]{:S(2)}) collective-permute-start(f32[2,32,1,128]{3,2,1,0:T(1,128)S(1)} %slice.106), channel_id=1, source_target_pairs={{0,1},{1,2},{2,3},{3,4},{4,5},{5,6},{6,7},{7,8},{8,9},{9,10},{10,1... | collective-permute-start | bytes 98312 | tf_op jit(solution)/shard_map/ppermute | solution.py:17
  40.0 0.2 slice.102
  40.2 1.9 collective-permute-start.2
  42.2 15.8 %collective-permute-done.2 = f32[2,32,16,1]{3,2,1,0:T(8,128)} collective-permute-done((f32[2,32,16,1]{3,2,1,0:T(8,128)S(1)}, f32[2,32,16,1]{3,2,1,0:T(8,128)}, u32[]{:S(2)}, u32[]{:S(2)}) %collective-permute-start.2) | collective-permute-done | bytes 4128 | tf_op jit(solution)/shard_map/ppermute | solution.py:11
  58.0 1.5 multiply_reduce_fusion.2
  59.5 0.2 dynamic-update-slice
  59.8 97.2 %all-reduce.7 = (f32[1024]{0:T(1024)S(1)}, f32[2]{0:T(128)S(1)}) all-reduce(f32[1024]{0:T(1024)S(1)} %dynamic-update-slice, f32[2]{0:T(128)S(1)} %get-tuple-element.2), channel_id=2, replica_groups=mesh['lon'=32,'lat'=16] {'lon','lat'}, use_global_device_ids=true, to_apply=%add.5 | all-reduce | flops 1026 | bytes 8208
  157.0 0.2 reshape.15
  157.3 0.3 multiply_reduce_fusion.1
  157.7 94.4 %all-reduce.6 = f32[1024]{0:T(1024)S(1)} all-reduce(f32[1024]{0:T(1024)S(1)} %dynamic-update-slice.1), channel_id=3, replica_groups=mesh['lon'=32,'lat'=16] {'lon','lat'}, use_global_device_ids=true, to_apply=%add.6 | all-reduce | flops 1024 | bytes 8192
  252.1 0.2 reshape.16
  252.6 2.6 collective-permute-start.8
  255.2 4.5 %collective-permute-start.6 = (f32[2,32,16,1]{3,2,1,0:T(8,128)S(1)}, f32[2,32,16,1]{3,2,1,0:T(8,128)S(1)}, u32[]{:S(2)}, u32[]{:S(2)}) collective-permute-start(f32[2,32,16,1]{3,2,1,0:T(8,128)S(1)} %bitcast.8), channel_id=1, source_target_pairs={{0,496},{16,0},{32,16},{48,32},{64,48},{80,64},{96,80},{112,96},{1... | collective-permute-start | bytes 12296 | tf_op jit(solution)/shard_map/ppermute | solution.py:11
  259.8 0.2 slice.110
  260.0 11.3 %collective-permute-done.6 = f32[2,32,16,1]{3,2,1,0:T(8,128)S(1)} collective-permute-done((f32[2,32,16,1]{3,2,1,0:T(8,128)S(1)}, f32[2,32,16,1]{3,2,1,0:T(8,128)S(1)}, u32[]{:S(2)}, u32[]{:S(2)}) %collective-permute-start.6) | collective-permute-done | bytes 4128 | tf_op jit(solution)/shard_map/ppermute | solution.py:11
  271.4 0.3 fusion.5
  271.8 2.6 collective-permute-start.9
  274.3 0.2 slice.112
  274.5 2.8 collective-permute-start.7
  277.4 15.8 %collective-permute-done.7 = f32[2,32,16,1]{3,2,1,0:T(8,128)S(1)} collective-permute-done((f32[2,32,16,1]{3,2,1,0:T(8,128)S(1)}, f32[2,32,16,1]{3,2,1,0:T(8,128)S(1)}, u32[]{:S(2)}, u32[]{:S(2)}) %collective-permute-start.7) | collective-permute-done | bytes 4128 | tf_op jit(solution)/shard_map/ppermute | solution.py:11
  293.2 0.5 multiply_reduce_fusion
  293.7 93.8 %psum.15 = f32[2]{0:T(128)S(1)} all-reduce(f32[2]{0:T(128)S(1)} %get-tuple-element.6), channel_id=1, replica_groups=mesh['lon'=32,'lat'=16] {'lon','lat'}, use_global_device_ids=true, to_apply=%region_7.0 | all-reduce | flops 2 | bytes 16 | tf_op jit(solution)/shard_map/psum | solution.py:75
  387.5 1.2 multiply_subtract_fusion
  (39 shorter events, 1.3 us)
Async XLA Ops:
  0.6 17.4 %copy-start = (f32[2,32,16,128]{3,2,1,0:T(8,128)S(1)}, f32[2,32,16,128]{3,2,1,0:T(8,128)}, u32[]{:S(2)}) copy-start(f32[2,32,16,128]{3,2,1,0:T(8,128)} %param.6) | copy-start | bytes 1572868
  1.7 22.4 %collective-permute-start.3 = (s32[32,1,128]{2,1,0:T(1,128)S(1)}, s32[32,1,128]{2,1,0:T(1,128)S(1)}, u32[]{:S(2)}, u32[]{:S(2)}) collective-permute-start(s32[32,1,128]{2,1,0:T(1,128)S(1)} %slice.105), channel_id=1, source_target_pairs={{1,0},{2,1},{3,2},{4,3},{5,4},{6,5},{7,6},{8,7},{9,8},{10,9},{11,1... | collective-permute-start | bytes 49160 | tf_op jit(solution)/shard_map/ppermute | solution.py:17
  10.5 13.6 %collective-permute-start = (s32[32,16,1]{2,1,0:T(8,128)S(1)}, s32[32,16,1]{2,1,0:T(8,128)S(1)}, u32[]{:S(2)}, u32[]{:S(2)}) collective-permute-start(s32[32,16,1]{2,1,0:T(8,128)S(1)} %bitcast.13), channel_id=1, source_target_pairs={{0,496},{16,0},{32,16},{48,32},{64,48},{80,64},{96,80},{112,96},{1... | collective-permute-start | bytes 6152 | tf_op jit(solution)/shard_map/ppermute | solution.py:11
  18.1 17.2 %collective-permute-start.4 = (f32[2,32,1,128]{3,2,1,0:T(1,128)S(1)}, f32[2,32,1,128]{3,2,1,0:T(1,128)S(1)}, u32[]{:S(2)}, u32[]{:S(2)}) collective-permute-start(f32[2,32,1,128]{3,2,1,0:T(1,128)S(1)} %slice.84), channel_id=1, source_target_pairs={{1,0},{2,1},{3,2},{4,3},{5,4},{6,5},{7,6},{8,7},{9,8},{10,9},{11,1... | collective-permute-start | bytes 98312 | tf_op jit(solution)/shard_map/ppermute | solution.py:17
  20.0 15.3 %collective-permute-start.1 = (f32[2,32,16,1]{3,2,1,0:T(8,128)S(1)}, f32[2,32,16,1]{3,2,1,0:T(8,128)S(1)}, u32[]{:S(2)}, u32[]{:S(2)}) collective-permute-start(f32[2,32,16,1]{3,2,1,0:T(8,128)S(1)} %bitcast.7), channel_id=1, source_target_pairs={{0,496},{16,0},{32,16},{48,32},{64,48},{80,64},{96,80},{112,96},{1... | collective-permute-start | bytes 12296 | tf_op jit(solution)/shard_map/ppermute | solution.py:11
  22.9 1.2 copy-start.1
  23.0 1.2 copy-start.2
  23.0 1.2 copy-start.3
  35.7 22.3 %collective-permute-start.5 = (f32[2,32,1,128]{3,2,1,0:T(1,128)S(1)}, f32[2,32,1,128]{3,2,1,0:T(1,128)S(1)}, u32[]{:S(2)}, u32[]{:S(2)}) collective-permute-start(f32[2,32,1,128]{3,2,1,0:T(1,128)S(1)} %slice.106), channel_id=1, source_target_pairs={{0,1},{1,2},{2,3},{3,4},{4,5},{5,6},{6,7},{7,8},{8,9},{9,10},{10,1... | collective-permute-start | bytes 98312 | tf_op jit(solution)/shard_map/ppermute | solution.py:17
  40.2 17.8 %collective-permute-start.2 = (f32[2,32,16,1]{3,2,1,0:T(8,128)S(1)}, f32[2,32,16,1]{3,2,1,0:T(8,128)}, u32[]{:S(2)}, u32[]{:S(2)}) collective-permute-start(f32[2,32,16,1]{3,2,1,0:T(8,128)S(1)} %slice.102), channel_id=1, source_target_pairs={{0,16},{16,32},{32,48},{48,64},{64,80},{80,96},{96,112},{112,128},... | collective-permute-start | bytes 12296 | tf_op jit(solution)/shard_map/ppermute | solution.py:11
  252.6 18.8 %collective-permute-start.8 = (f32[2,32,1,128]{3,2,1,0:T(1,128)S(1)}, f32[2,32,1,128]{3,2,1,0:T(1,128)S(1)}, u32[]{:S(2)}, u32[]{:S(2)}) collective-permute-start(f32[2,32,1,128]{3,2,1,0:T(1,128)S(1)} %slice.115), channel_id=1, source_target_pairs={{1,0},{2,1},{3,2},{4,3},{5,4},{6,5},{7,6},{8,7},{9,8},{10,9},{11,1... | collective-permute-start | bytes 98312 | tf_op jit(solution)/shard_map/ppermute | solution.py:17
  255.2 16.2 %collective-permute-start.6 = (f32[2,32,16,1]{3,2,1,0:T(8,128)S(1)}, f32[2,32,16,1]{3,2,1,0:T(8,128)S(1)}, u32[]{:S(2)}, u32[]{:S(2)}) collective-permute-start(f32[2,32,16,1]{3,2,1,0:T(8,128)S(1)} %bitcast.8), channel_id=1, source_target_pairs={{0,496},{16,0},{32,16},{48,32},{64,48},{80,64},{96,80},{112,96},{1... | collective-permute-start | bytes 12296 | tf_op jit(solution)/shard_map/ppermute | solution.py:11
  271.8 21.4 %collective-permute-start.9 = (f32[2,32,1,128]{3,2,1,0:T(1,128)S(1)}, f32[2,32,1,128]{3,2,1,0:T(1,128)S(1)}, u32[]{:S(2)}, u32[]{:S(2)}) collective-permute-start(f32[2,32,1,128]{3,2,1,0:T(1,128)S(1)} %slice.116), channel_id=1, source_target_pairs={{0,1},{1,2},{2,3},{3,4},{4,5},{5,6},{6,7},{7,8},{8,9},{9,10},{10,1... | collective-permute-start | bytes 98312 | tf_op jit(solution)/shard_map/ppermute | solution.py:17
  274.5 18.7 %collective-permute-start.7 = (f32[2,32,16,1]{3,2,1,0:T(8,128)S(1)}, f32[2,32,16,1]{3,2,1,0:T(8,128)S(1)}, u32[]{:S(2)}, u32[]{:S(2)}) collective-permute-start(f32[2,32,16,1]{3,2,1,0:T(8,128)S(1)} %slice.112), channel_id=1, source_target_pairs={{0,16},{16,32},{32,48},{48,64},{64,80},{80,96},{96,112},{112,128},... | collective-permute-start | bytes 12296 | tf_op jit(solution)/shard_map/ppermute | solution.py:11
